TPU v7x, 32 devices: a whole 2x2x4 slice. The times are simulated.
32 devices in a mesh: det: 4 (over y, x), obs: 8 (over z, core).
Axes of the slice: x: 2, y: 2, z: 4, core: 2. Of those that a mesh axis runs over, the one named last changes fastest.
Arguments:
- tod: float32 [4, 8, 8192], P('det', 'obs'), may hold values from -200 to 200
- angle: float32 [4, 8, 8192], P('det', 'obs'), may hold values from -3.140625 to 3.140625
- pix_in: int32 [4, 8, 8192], P('det', 'obs'), may hold values from 0 to 63
- tile_block: int32 [4, 8, 32], P('det', 'obs'), may hold values from 0 to 511
- base_len: int32 [4, 8, 40], P('det', 'obs'), may hold values from 1 to 384, 8192 in all within a row
- touched: int32 [8, 16], P('obs'), may hold values from 0 to 511, as said below
Outputs:
- baselines: float32 [4, 8, 40], P('det', 'obs')
- residual_rate: float32 [4, 8, 40], P('det', 'obs')
Inputs may be any that keep to these rules, and one draw needn't show every extreme that they name: `touched`: each row lists 16 distinct patches; patch p is held by owner p // 64; at most 4 patches of one row share an owner, and one owner holds exactly 4 patches of every row.
All inputs are finite; a program needn't handle non-finite values.
Results may differ from a plain program's by a relative error of at most 0.0003.
Values sent between devices are 32-bit elements; how exact they have to be, the bound alone decides.
A program may use at most 128 MiB of HBM per device.

v0:
```python
import math
import jax
import jax.numpy as jnp
from jax import lax
from jax.sharding import PartitionSpec as P

TILE = 256
BLK = 64
PATCH_PIX = 2048
PT = 16
PATCH_OWN = 64
ITERS = 2
UPPER_LIMIT = lax.Precision.HIGHEST


def pixel_inverse(hits):
    a11 = hits[:, 0] + 1.0
    a12 = hits[:, 1]
    a13 = hits[:, 2]
    a22 = hits[:, 3] + 1.0
    a23 = hits[:, 4]
    a33 = hits[:, 5] + 1.0
    c11 = a22 * a33 - a23 * a23
    c12 = a13 * a23 - a12 * a33
    c13 = a12 * a23 - a13 * a22
    c22 = a11 * a33 - a13 * a13
    c23 = a12 * a13 - a11 * a23
    c33 = a11 * a22 - a12 * a12
    determinant = a11 * c11 + a12 * c12 + a13 * c13
    return jnp.stack([c11, c12, c13, c22, c23, c33], axis=1) / determinant[:, None]


def apply_inverse(inverse, pixel_binned_map):
    first = (
        inverse[:, 0] * pixel_binned_map[:, 0]
        + inverse[:, 1] * pixel_binned_map[:, 1]
        + inverse[:, 2] * pixel_binned_map[:, 2]
    )
    second = (
        inverse[:, 1] * pixel_binned_map[:, 0]
        + inverse[:, 3] * pixel_binned_map[:, 1]
        + inverse[:, 4] * pixel_binned_map[:, 2]
    )
    third = (
        inverse[:, 2] * pixel_binned_map[:, 0]
        + inverse[:, 4] * pixel_binned_map[:, 1]
        + inverse[:, 5] * pixel_binned_map[:, 2]
    )
    return jnp.stack([first, second, third], axis=1)


def combine_det(partial_value):
    total = lax.psum(partial_value, "det")
    return total


def squares(residual_vector):
    return lax.psum(jnp.sum(residual_vector * residual_vector), ("det", "obs"))


def body(tod, angle, pix_in, tile_block, base_len, touched):
    signal = tod[0, 0]
    inner = pix_in[0, 0]
    tile_rows = tile_block[0, 0]
    lengths = base_len[0, 0]
    patch_list = touched[0]
    samples = signal.shape[0]
    nbase = lengths.shape[0]
    ntile = samples // TILE
    group = math.gcd(ntile, 64)
    groups = ntile // group
    blocks = PATCH_PIX // BLK
    local_blocks = PT * blocks
    obs_count = lax.axis_size("obs")
    cap = max(2, 2 * PT // obs_count)
    slots = obs_count * cap
    cos_w = jnp.cos(2.0 * angle[0, 0])
    sin_w = jnp.sin(2.0 * angle[0, 0])
    ends = jnp.cumsum(lengths)
    base_index = jnp.searchsorted(ends, jnp.arange(samples, dtype=jnp.int32), side="right")
    inner_groups = inner.reshape(groups, group, TILE)
    cos_groups = cos_w.reshape(groups, group, TILE)
    sin_groups = sin_w.reshape(groups, group, TILE)
    pixel_iota = jnp.arange(BLK, dtype=jnp.int32)
    tile_select = (tile_rows[None, :] == jnp.arange(local_blocks, dtype=jnp.int32)[:, None]).astype(
        jnp.float32
    )

    def tile_indicator_matrix(index):
        return (index[:, None, :] == pixel_iota[None, :, None]).astype(jnp.float32)

    def bin_local(value_entries):
        comps = value_entries.shape[0]
        grouped = value_entries.reshape(comps, groups, group, TILE).transpose(1, 2, 0, 3)

        def bin_one_group(index_couple):
            return jnp.einsum(
                "awv,agv->awg",
                index_couple[0],
                tile_indicator_matrix(index_couple[1]),
                precision=UPPER_LIMIT,
            )

        per_tile = lax.map(bin_one_group, (grouped, inner_groups)).reshape(ntile, comps * BLK)
        summed = jnp.dot(tile_select, per_tile, precision=UPPER_LIMIT)
        return (
            summed.reshape(PT, blocks, comps, BLK)
            .transpose(0, 2, 1, 3)
            .reshape(PT, comps, PATCH_PIX)
        )

    def unbin_local(local_map):
        rows = (
            local_map.reshape(PT, 3, blocks, BLK)
            .transpose(0, 2, 1, 3)
            .reshape(local_blocks, 3 * BLK)
        )
        picked = jnp.take(rows, tile_rows, axis=0).reshape(groups, group, 3, BLK)

        def unbin_one_group(partition_pieces):
            value_entries = jnp.einsum(
                "jwx,jxd->jwd",
                partition_pieces[0],
                tile_indicator_matrix(partition_pieces[1]),
                precision=UPPER_LIMIT,
            )
            return (
                value_entries[:, 0]
                + partition_pieces[2] * value_entries[:, 1]
                + partition_pieces[3] * value_entries[:, 2]
            )

        return lax.map(unbin_one_group, (picked, inner_groups, cos_groups, sin_groups)).reshape(
            samples
        )

    owner_of = patch_list // PATCH_OWN
    slot_of = patch_list % PATCH_OWN
    positions = jnp.arange(PT, dtype=jnp.int32)
    before = (owner_of[None, :] == owner_of[:, None]) & (positions[None, :] < positions[:, None])
    rank = jnp.sum(before.astype(jnp.int32), axis=1)
    target = owner_of * cap + rank
    placed = target[None, :] == jnp.arange(slots, dtype=jnp.int32)[:, None]
    packing = placed.astype(jnp.float32)
    send_ids = (jnp.sum(jnp.where(placed, slot_of[None, :] + 1, 0), axis=1) - 1).reshape(
        obs_count, cap
    )

    def pack_map(total):
        comps, width = (total.shape[1], total.shape[2])
        return jnp.dot(packing, total.reshape(PT, comps * width), precision=UPPER_LIMIT).reshape(
            obs_count, cap, comps, width
        )

    def unpack_map(returned):
        width = returned.shape[3]
        return jnp.dot(
            packing.T, returned.reshape(slots, 3 * width), precision=UPPER_LIMIT
        ).reshape(PT, 3, width)

    ones = jnp.ones_like(signal)
    first_values = jnp.stack(
        [
            signal,
            signal * cos_w,
            signal * sin_w,
            ones,
            cos_w,
            sin_w,
            cos_w * cos_w,
            cos_w * sin_w,
            sin_w * sin_w,
        ]
    )
    first_total = combine_det(bin_local(first_values))
    received, source_ids = (
        lax.all_to_all(pack_map(first_total), "obs", split_axis=0, concat_axis=0, tiled=True),
        lax.all_to_all(send_ids, "obs", split_axis=0, concat_axis=0, tiled=True),
    )
    owner_pick = (
        source_ids.reshape(slots)[None, :] == jnp.arange(PATCH_OWN, dtype=jnp.int32)[:, None]
    ).astype(jnp.float32)

    def gather_owner(arrived):
        comps, width = (arrived.shape[2], arrived.shape[3])
        return jnp.dot(
            owner_pick, arrived.reshape(slots, comps * width), precision=UPPER_LIMIT
        ).reshape(PATCH_OWN, comps, width)

    def return_map(owned):
        width = owned.shape[2]
        outgoing = jnp.dot(
            owner_pick.T, owned.reshape(PATCH_OWN, 3 * width), precision=UPPER_LIMIT
        ).reshape(obs_count, cap, 3, width)
        return lax.all_to_all(outgoing, "obs", split_axis=0, concat_axis=0, tiled=True)

    accumulated = gather_owner(received)
    inverse = pixel_inverse(accumulated[:, 3:])
    start_map = apply_inverse(inverse, accumulated[:, :3])
    start_local = unpack_map(return_map(start_map))
    cleaned = signal - unbin_local(start_local)
    right_side = jax.ops.segment_sum(
        cleaned, base_index, num_segments=nbase, indices_are_sorted=True
    )
    solution = jnp.zeros_like(right_side)
    residual_vector = right_side
    direction = right_side
    norm_now = squares(residual_vector)
    for step in range(ITERS):
        expanded = jnp.take(direction, base_index)
        apply_value_entries = jnp.stack([expanded, expanded * cos_w, expanded * sin_w])
        apply_total = combine_det(bin_local(apply_value_entries))
        apply_arrived = lax.all_to_all(
            pack_map(apply_total), "obs", split_axis=0, concat_axis=0, tiled=True
        )
        solved = apply_inverse(inverse, gather_owner(apply_arrived))
        apply_local_map = unpack_map(return_map(solved))
        image = jax.ops.segment_sum(
            expanded - unbin_local(apply_local_map),
            base_index,
            num_segments=nbase,
            indices_are_sorted=True,
        )
        alpha = norm_now / lax.psum(jnp.sum(direction * image), ("det", "obs"))
        solution = solution + alpha * direction
        residual_vector = residual_vector - alpha * image
        if step + 1 < ITERS:
            norm_next = squares(residual_vector)
            direction = residual_vector + norm_next / norm_now * direction
            norm_now = norm_next
    rate = residual_vector / lengths.astype(jnp.float32)
    return (solution[None, None], rate[None, None])


def solution(mesh):
    placed = (
        P("det", "obs", None),
        P("det", "obs", None),
        P("det", "obs", None),
        P("det", "obs", None),
        P("det", "obs", None),
        P("obs", None),
    )
    return jax.shard_map(
        body,
        mesh=mesh,
        in_specs=placed,
        out_specs=(P("det", "obs", None), P("det", "obs", None)),
        check_vma=False,
    )
```

profile of v0, /device:TPU:12, one launch (start us, length us, event | category | flops | bytes accessed | tf_op | source)
XLA Modules:
  0.0 1070.5 jit_solution(13468639081524979222)
XLA Ops:
  18.3 5.3 all-to-all-start
  23.7 49.2 %all-reduce.5.cloned.1.call-done = f32[9,2048,16]{1,2,0:T(8,128)} async-done(((f32[9,2048,16]{1,2,0:T(8,128)}), f32[9,2048,16]{1,2,0:T(8,128)}) %all-reduce.5.cloned.1.call-update) | async-done | bytes 1179664 | tf_op jit(solution)/shard_map/psum | solution.py:53
  77.3 5.8 all-to-all-start.1
  84.3 50.0 %all-to-all-done.1 = f32[8,4,9,2048]{3,1,2,0:T(4,128)S(1)} async-done(((f32[8,4,9,2048]{3,1,2,0:T(4,128)}), f32[8,4,9,2048]{3,1,2,0:T(4,128)S(1)}, u32[]{:S(2)}, u32[]{:S(2)}) %all-to-all-start.1) | async-done | bytes 2359328 | tf_op jit(solution)/shard_map/all_to_all | solution.py:177
  142.9 7.5 all-to-all-start.2
  150.6 312.5 %while.24 = (s32[]{:T(128)}, u32[8192]{0:T(1024)S(1)}, u32[8192]{0:T(1024)S(1)}, s32[40]{0:T(128)S(1)}, s32[]{:T(128)}, /*index=5*/s32[]{:T(128)}) while((s32[]{:T(128)}, u32[8192]{0:T(1024)S(1)}, u32[8192]{0:T(1024)S(1)}, s32[40]{0:T(128)S(1)}, s32[]{:T(128)}, /*index=5*/s32[]{:T(128)}) %tuple.233), condition=%wide.region_2.3_spmd.clone, body=%wide.region_1.2_spmd.clone.sunk | while | flops 1392643 | bytes 262864 | solution.py:80
  152.8 25.0 %fusion.141 = u32[8192]{0:T(1024)S(1)} fusion(u32[8192]{0:T(1024)S(1)} %get-tuple-element.525, u32[8192]{0:T(1024)S(1)} %get-tuple-element.524, s32[]{:T(128)} %bitcast.438, s32[]{:T(128)} %bitcast.439, s32[]{:T(128)} %bitcast.440, s32[]{:T(128)} %bitcast.441, s32[]{:T(128)} %bitcast.442, s32[]{:T(128)} %bitcast.443, s32[]{:T(128)} %bitcast.444, ...), kind=kLoop, calls=%fused_computation.8.clone.1 | loop fusion | flops 696320 | bytes 98465 | tf_op jit(solution)/shard_map/jit(searchsorted)/jit(_searchsorted_scan_impl)/vmap(jit(_searchsorted_scan_impl))/while/body/eval_jaxpr/select_n | solution.py:80
  177.7 25.0 %fusion.140 = u32[8192]{0:T(1024)S(1)} fusion(u32[8192]{0:T(1024)S(1)} %get-tuple-element.525, u32[8192]{0:T(1024)S(1)} %get-tuple-element.524, s32[]{:T(128)} %bitcast.438, s32[]{:T(128)} %bitcast.439, s32[]{:T(128)} %bitcast.440, s32[]{:T(128)} %bitcast.441, s32[]{:T(128)} %bitcast.442, s32[]{:T(128)} %bitcast.443, s32[]{:T(128)} %bitcast.444, ...), kind=kLoop, calls=%fused_computation.9.clone.1 | loop fusion | flops 696320 | bytes 98465 | tf_op jit(solution)/shard_map/jit(searchsorted)/jit(_searchsorted_scan_impl)/vmap(jit(_searchsorted_scan_impl))/while/body/eval_jaxpr/select_n | solution.py:80
  204.9 25.0 %fusion.141 = u32[8192]{0:T(1024)S(1)} fusion(u32[8192]{0:T(1024)S(1)} %get-tuple-element.525, u32[8192]{0:T(1024)S(1)} %get-tuple-element.524, s32[]{:T(128)} %bitcast.438, s32[]{:T(128)} %bitcast.439, s32[]{:T(128)} %bitcast.440, s32[]{:T(128)} %bitcast.441, s32[]{:T(128)} %bitcast.442, s32[]{:T(128)} %bitcast.443, s32[]{:T(128)} %bitcast.444, ...), kind=kLoop, calls=%fused_computation.8.clone.1 | loop fusion | flops 696320 | bytes 98465 | tf_op jit(solution)/shard_map/jit(searchsorted)/jit(_searchsorted_scan_impl)/vmap(jit(_searchsorted_scan_impl))/while/body/eval_jaxpr/select_n | solution.py:80
  229.8 25.0 %fusion.140 = u32[8192]{0:T(1024)S(1)} fusion(u32[8192]{0:T(1024)S(1)} %get-tuple-element.525, u32[8192]{0:T(1024)S(1)} %get-tuple-element.524, s32[]{:T(128)} %bitcast.438, s32[]{:T(128)} %bitcast.439, s32[]{:T(128)} %bitcast.440, s32[]{:T(128)} %bitcast.441, s32[]{:T(128)} %bitcast.442, s32[]{:T(128)} %bitcast.443, s32[]{:T(128)} %bitcast.444, ...), kind=kLoop, calls=%fused_computation.9.clone.1 | loop fusion | flops 696320 | bytes 98465 | tf_op jit(solution)/shard_map/jit(searchsorted)/jit(_searchsorted_scan_impl)/vmap(jit(_searchsorted_scan_impl))/while/body/eval_jaxpr/select_n | solution.py:80
  256.9 25.0 %fusion.141 = u32[8192]{0:T(1024)S(1)} fusion(u32[8192]{0:T(1024)S(1)} %get-tuple-element.525, u32[8192]{0:T(1024)S(1)} %get-tuple-element.524, s32[]{:T(128)} %bitcast.438, s32[]{:T(128)} %bitcast.439, s32[]{:T(128)} %bitcast.440, s32[]{:T(128)} %bitcast.441, s32[]{:T(128)} %bitcast.442, s32[]{:T(128)} %bitcast.443, s32[]{:T(128)} %bitcast.444, ...), kind=kLoop, calls=%fused_computation.8.clone.1 | loop fusion | flops 696320 | bytes 98465 | tf_op jit(solution)/shard_map/jit(searchsorted)/jit(_searchsorted_scan_impl)/vmap(jit(_searchsorted_scan_impl))/while/body/eval_jaxpr/select_n | solution.py:80
  281.9 25.0 %fusion.140 = u32[8192]{0:T(1024)S(1)} fusion(u32[8192]{0:T(1024)S(1)} %get-tuple-element.525, u32[8192]{0:T(1024)S(1)} %get-tuple-element.524, s32[]{:T(128)} %bitcast.438, s32[]{:T(128)} %bitcast.439, s32[]{:T(128)} %bitcast.440, s32[]{:T(128)} %bitcast.441, s32[]{:T(128)} %bitcast.442, s32[]{:T(128)} %bitcast.443, s32[]{:T(128)} %bitcast.444, ...), kind=kLoop, calls=%fused_computation.9.clone.1 | loop fusion | flops 696320 | bytes 98465 | tf_op jit(solution)/shard_map/jit(searchsorted)/jit(_searchsorted_scan_impl)/vmap(jit(_searchsorted_scan_impl))/while/body/eval_jaxpr/select_n | solution.py:80
  309.0 25.0 %fusion.141 = u32[8192]{0:T(1024)S(1)} fusion(u32[8192]{0:T(1024)S(1)} %get-tuple-element.525, u32[8192]{0:T(1024)S(1)} %get-tuple-element.524, s32[]{:T(128)} %bitcast.438, s32[]{:T(128)} %bitcast.439, s32[]{:T(128)} %bitcast.440, s32[]{:T(128)} %bitcast.441, s32[]{:T(128)} %bitcast.442, s32[]{:T(128)} %bitcast.443, s32[]{:T(128)} %bitcast.444, ...), kind=kLoop, calls=%fused_computation.8.clone.1 | loop fusion | flops 696320 | bytes 98465 | tf_op jit(solution)/shard_map/jit(searchsorted)/jit(_searchsorted_scan_impl)/vmap(jit(_searchsorted_scan_impl))/while/body/eval_jaxpr/select_n | solution.py:80
  334.0 25.0 %fusion.140 = u32[8192]{0:T(1024)S(1)} fusion(u32[8192]{0:T(1024)S(1)} %get-tuple-element.525, u32[8192]{0:T(1024)S(1)} %get-tuple-element.524, s32[]{:T(128)} %bitcast.438, s32[]{:T(128)} %bitcast.439, s32[]{:T(128)} %bitcast.440, s32[]{:T(128)} %bitcast.441, s32[]{:T(128)} %bitcast.442, s32[]{:T(128)} %bitcast.443, s32[]{:T(128)} %bitcast.444, ...), kind=kLoop, calls=%fused_computation.9.clone.1 | loop fusion | flops 696320 | bytes 98465 | tf_op jit(solution)/shard_map/jit(searchsorted)/jit(_searchsorted_scan_impl)/vmap(jit(_searchsorted_scan_impl))/while/body/eval_jaxpr/select_n | solution.py:80
  361.1 25.0 %fusion.141 = u32[8192]{0:T(1024)S(1)} fusion(u32[8192]{0:T(1024)S(1)} %get-tuple-element.525, u32[8192]{0:T(1024)S(1)} %get-tuple-element.524, s32[]{:T(128)} %bitcast.438, s32[]{:T(128)} %bitcast.439, s32[]{:T(128)} %bitcast.440, s32[]{:T(128)} %bitcast.441, s32[]{:T(128)} %bitcast.442, s32[]{:T(128)} %bitcast.443, s32[]{:T(128)} %bitcast.444, ...), kind=kLoop, calls=%fused_computation.8.clone.1 | loop fusion | flops 696320 | bytes 98465 | tf_op jit(solution)/shard_map/jit(searchsorted)/jit(_searchsorted_scan_impl)/vmap(jit(_searchsorted_scan_impl))/while/body/eval_jaxpr/select_n | solution.py:80
  386.1 25.0 %fusion.140 = u32[8192]{0:T(1024)S(1)} fusion(u32[8192]{0:T(1024)S(1)} %get-tuple-element.525, u32[8192]{0:T(1024)S(1)} %get-tuple-element.524, s32[]{:T(128)} %bitcast.438, s32[]{:T(128)} %bitcast.439, s32[]{:T(128)} %bitcast.440, s32[]{:T(128)} %bitcast.441, s32[]{:T(128)} %bitcast.442, s32[]{:T(128)} %bitcast.443, s32[]{:T(128)} %bitcast.444, ...), kind=kLoop, calls=%fused_computation.9.clone.1 | loop fusion | flops 696320 | bytes 98465 | tf_op jit(solution)/shard_map/jit(searchsorted)/jit(_searchsorted_scan_impl)/vmap(jit(_searchsorted_scan_impl))/while/body/eval_jaxpr/select_n | solution.py:80
  413.2 25.0 %fusion.141 = u32[8192]{0:T(1024)S(1)} fusion(u32[8192]{0:T(1024)S(1)} %get-tuple-element.525, u32[8192]{0:T(1024)S(1)} %get-tuple-element.524, s32[]{:T(128)} %bitcast.438, s32[]{:T(128)} %bitcast.439, s32[]{:T(128)} %bitcast.440, s32[]{:T(128)} %bitcast.441, s32[]{:T(128)} %bitcast.442, s32[]{:T(128)} %bitcast.443, s32[]{:T(128)} %bitcast.444, ...), kind=kLoop, calls=%fused_computation.8.clone.1 | loop fusion | flops 696320 | bytes 98465 | tf_op jit(solution)/shard_map/jit(searchsorted)/jit(_searchsorted_scan_impl)/vmap(jit(_searchsorted_scan_impl))/while/body/eval_jaxpr/select_n | solution.py:80
  438.2 25.0 %fusion.140 = u32[8192]{0:T(1024)S(1)} fusion(u32[8192]{0:T(1024)S(1)} %get-tuple-element.525, u32[8192]{0:T(1024)S(1)} %get-tuple-element.524, s32[]{:T(128)} %bitcast.438, s32[]{:T(128)} %bitcast.439, s32[]{:T(128)} %bitcast.440, s32[]{:T(128)} %bitcast.441, s32[]{:T(128)} %bitcast.442, s32[]{:T(128)} %bitcast.443, s32[]{:T(128)} %bitcast.444, ...), kind=kLoop, calls=%fused_computation.9.clone.1 | loop fusion | flops 696320 | bytes 98465 | tf_op jit(solution)/shard_map/jit(searchsorted)/jit(_searchsorted_scan_impl)/vmap(jit(_searchsorted_scan_impl))/while/body/eval_jaxpr/select_n | solution.py:80
  479.4 57.2 %scatter_custom_fusion = f32[40]{0:T(128)S(1)} fusion(s32[8192]{0:T(1024)} %convert_element_type.34, f32[8192]{0:T(1024)S(1)} %add_subtract_fusion.2, f32[]{:T(128)} %constant.148.clone.1), kind=kCustom, calls=%fused_computation.230 | custom fusion | flops 8192 | bytes 672 | tf_op jit(solution)/shard_map/scatter-add | solution.py:202
  538.6 25.7 %fusion.114 = (f32[8192]{0:T(1024)S(1)}, f32[8192]{0:T(1024)S(1)}, pred[8192]{0:T(1024)(128)(4,1)S(1)}, pred[8192]{0:T(1024)(128)(4,1)S(1)}, pred[8192]{0:T(1024...) fusion(f32[8192]{0:T(1024)S(1)} %bitcast.499, ...), kind=kLoop, calls=%fused_computation.235 | loop fusion | flops 712704 | bytes 458912 | tf_op jit(solution)/shard_map/mul | solution.py:211
  571.7 44.1 %all-reduce.7.cloned.1.call-done = f32[3,2048,16]{1,2,0:T(8,128)} async-done(((f32[3,2048,16]{1,2,0:T(8,128)}), f32[3,2048,16]{1,2,0:T(8,128)}) %all-reduce.7.cloned.1.call-update) | async-done | bytes 393232 | tf_op jit(solution)/shard_map/psum | solution.py:53
  617.4 23.8 %all_to_all.36 = f32[8,4,3,2048]{3,1,2,0:T(4,128)S(1)} all-to-all(f32[8,4,3,2048]{3,1,2,0:T(4,128)S(1)} %fusion.51), channel_id=1, replica_groups=mesh['det'=4,'obs'=8] {'obs'}, dimensions={0} | all-to-all | bytes 1572864 | tf_op jit(solution)/shard_map/all_to_all | solution.py:213
  644.5 23.4 %all_to_all.37 = f32[8,4,3,2048]{3,1,2,0:T(4,128)S(1)} all-to-all(f32[8,4,3,2048]{3,1,2,0:T(4,128)S(1)} %fusion.15), channel_id=1, replica_groups=mesh['det'=4,'obs'=8] {'obs'}, dimensions={0} | all-to-all | bytes 1572864 | tf_op jit(solution)/shard_map/all_to_all | solution.py:195
  682.4 57.2 %scatter_custom_fusion.1 = f32[40]{0:T(128)S(1)} fusion(s32[8192]{0:T(1024)} %convert_element_type.34, f32[8192]{0:T(1024)S(1)} %add_subtract_fusion.1, f32[]{:T(128)} %constant.148.clone.1), kind=kCustom, calls=%fused_computation.228 | custom fusion | flops 8192 | bytes 672 | tf_op jit(solution)/shard_map/scatter-add | solution.py:218
  740.1 41.3 %all-reduce = (f32[]{:T(128)}, f32[]{:T(128)}) all-reduce(f32[]{:T(128)} %get-tuple-element.196, f32[]{:T(128)} %get-tuple-element.195), channel_id=1, replica_groups=mesh['det'=4,'obs'=8] {'det','obs'}, use_global_device_ids=true, to_apply=%region_8.10 | all-reduce | flops 2 | bytes 16 | tf_op jit(solution)/shard_map/psum | solution.py:58
  783.4 39.9 %psum.53 = f32[]{:T(128)} all-reduce(f32[]{:T(128)} %get-tuple-element.209), channel_id=1, replica_groups=mesh['det'=4,'obs'=8] {'det','obs'}, use_global_device_ids=true, to_apply=%region_14.17 | all-reduce | flops 1 | bytes 8 | tf_op jit(solution)/shard_map/psum | solution.py:58
  826.7 25.8 %fusion.113 = (f32[8192]{0:T(1024)S(1)}, f32[8192]{0:T(1024)S(1)}) fusion(f32[8192]{0:T(1024)S(1)} %bitcast.501, pred[8192]{0:T(1024)(128)(4,1)} %get-tuple-element.252, pred[8192]{0:T(1024)(128)(4,1)} %get-tuple-element.251, pred[8192]{0:T(1024)(128)(4,1)} %get-tuple-element.250, pred[8192]{0:T(1024)(128)(4,1)} %get-tuple-element.249, ...), kind=kLoop, calls=%fused_computation.234 | loop fusion | flops 335872 | bytes 426144 | tf_op jit(solution)/shard_map/mul | solution.py:211
  859.8 44.0 %all-reduce.9.cloned.1.call-done = f32[3,2048,16]{1,2,0:T(8,128)} async-done(((f32[3,2048,16]{1,2,0:T(8,128)}), f32[3,2048,16]{1,2,0:T(8,128)}) %all-reduce.9.cloned.1.call-update) | async-done | bytes 393232 | tf_op jit(solution)/shard_map/psum | solution.py:53
  905.4 23.6 %all_to_all.38 = f32[8,4,3,2048]{3,1,2,0:T(4,128)S(1)} all-to-all(f32[8,4,3,2048]{3,1,2,0:T(4,128)S(1)} %fusion.49), channel_id=1, replica_groups=mesh['det'=4,'obs'=8] {'obs'}, dimensions={0} | all-to-all | bytes 1572864 | tf_op jit(solution)/shard_map/all_to_all | solution.py:213
  932.2 23.6 %all_to_all.39 = f32[8,4,3,2048]{3,1,2,0:T(4,128)S(1)} all-to-all(f32[8,4,3,2048]{3,1,2,0:T(4,128)S(1)} %fusion.13), channel_id=1, replica_groups=mesh['det'=4,'obs'=8] {'obs'}, dimensions={0} | all-to-all | bytes 1572864 | tf_op jit(solution)/shard_map/all_to_all | solution.py:195
  962.1 57.2 %scatter_custom_fusion.2 = f32[40]{0:T(128)S(1)} fusion(s32[8192]{0:T(1024)} %convert_element_type.34, f32[8192]{0:T(1024)S(1)} %add_subtract_fusion, f32[]{:T(128)} %constant.148.clone.1), kind=kCustom, calls=%fused_computation.226 | custom fusion | flops 8192 | bytes 672 | tf_op jit(solution)/shard_map/scatter-add | solution.py:218
  1019.9 41.3 %psum.55 = f32[]{:T(128)} all-reduce(f32[]{:T(128)} %multiply_reduce_fusion), channel_id=1, replica_groups=mesh['det'=4,'obs'=8] {'det','obs'}, use_global_device_ids=true, to_apply=%region_18.21 | all-reduce | flops 1 | bytes 8 | tf_op jit(solution)/shard_map/psum | solution.py:224
  (188 shorter events, 106.0 us)
Async XLA Ops:
  7.2 7.1 copy-start.14
  7.2 65.7 %all-reduce.5.cloned.1.call-start = ((), (), s32[]{:S(2)}) async-start(), calls=%async_computation.7 | async-start | bytes 2359296 | tf_op jit(solution)/shard_map/psum | solution.py:53
  8.9 5.3 copy-start
  8.9 5.3 copy-start.2
  11.0 3.3 copy-start.5
  16.2 1.1 copy-start.17
  17.5 452.3 %copy-start.7 = (s32[16]{0:T(128)}, s32[16]{0:T(128)S(1)}, u32[]{:S(2)}) copy-start(s32[16]{0:T(128)S(1)} %fusion.103) | copy-start | bytes 196
  18.3 59.0 %all-to-all-start = ((s32[8,1,4]{2,1,0:T(1,128)}), s32[8,1,4]{2,1,0:T(1,128)S(1)}, u32[]{:S(2)}, u32[]{:S(2)}) async-start(s32[8,1,4]{2,1,0:T(1,128)} %bitcast.10), calls=%async_computation | async-start | bytes 8192 | tf_op jit(solution)/shard_map/all_to_all | solution.py:178
  77.3 5.9 copy-start.15
  77.3 57.0 %all-to-all-start.1 = ((f32[8,4,9,2048]{3,1,2,0:T(4,128)}), f32[8,4,9,2048]{3,1,2,0:T(4,128)S(1)}, u32[]{:S(2)}, u32[]{:S(2)}) async-start(f32[8,4,9,2048]{3,1,2,0:T(4,128)} %fusion.34), calls=%async_computation.1 | async-start | bytes 4718592 | tf_op jit(solution)/shard_map/all_to_all | solution.py:177
  142.9 320.9 %all-to-all-start.2 = ((f32[8,4,3,2048]{3,1,2,0:T(4,128)}), f32[8,4,3,2048]{3,1,2,0:T(4,128)}, u32[]{:S(2)}, u32[]{:S(2)}) async-start(f32[8,4,3,2048]{3,1,2,0:T(4,128)} %fusion.17), calls=%async_computation.2 | async-start | bytes 1572864 | tf_op jit(solution)/shard_map/all_to_all | solution.py:195
  150.5 465.4 %all-reduce.7.cloned.1.call-start = ((), (), s32[]{:S(2)}) async-start(), calls=%async_computation.8 | async-start | bytes 786432 | tf_op jit(solution)/shard_map/psum | solution.py:53
  463.8 12.8 %copy-start.10 = (s32[1024]{0:T(1024)}, s32[1024]{0:T(1024)S(1)}, u32[]{:S(2)}) copy-start(s32[1024]{0:T(1024)S(1)} %pad_clamp_fusion) | copy-start | bytes 12292
  463.8 14.5 %copy-start.11 = (pred[32]{0:T(512)(128)(4,1)}, pred[32]{0:T(512)(128)(4,1)S(1)}, u32[]{:S(2)}) copy-start(pred[32]{0:T(512)(128)(4,1)S(1)} %compare_and_fusion.1) | copy-start | bytes 100
  472.7 5.8 copy-start.6
  472.7 6.6 copy-start.1
  472.7 6.6 copy-start.3
  472.7 6.6 copy-start.4
  571.6 332.2 %all-reduce.9.cloned.1.call-start = ((), (), s32[]{:S(2)}) async-start(), calls=%async_computation.9 | async-start | bytes 786432 | tf_op jit(solution)/shard_map/psum | solution.py:53
  668.4 4.3 copy-start.8
  675.6 5.7 copy-start.12
  956.5 1.1 copy-start.9
  959.2 1.9 copy-start.13
  959.2 103.3 %copy-start.16 = (s32[1,1,40]{2,1,0:T(1,128)S(1)}, s32[1,1,40]{2,1,0:T(1,128)}, u32[]{:S(2)}) copy-start(s32[1,1,40]{2,1,0:T(1,128)} %param.16) | copy-start | bytes 484
Sparse Core Ops, SparseCore 0:
  17.4 55.4 all-reduce.4
  571.8 44.0 all-reduce.6
  860.0 43.8 all-reduce.8
where the time goes:
time: 1080 us; the launch traced here: 1070 us
  other arithmetic  534 us (49%)
  blocking collectives  217 us (20%)
  waiting for transfers between devices  187 us (17%)
  local copies, waits for them, and re-layouts  58.7 us (5%)
  matrix products  35.6 us (3%)
  between operations  19 us (2%)
  starting transfers between devices  18.9 us (2%)
    select_n x12, other arithmetic, body(): jnp.searchsorted(ends, jnp.arange(samples, dtype=jnp.int32), side='right')  300 us
    psum x3, waiting for transfers between devices, combine_det(): total = lax.psum(partial_value, 'det')  137 us
    scatter-add x2, other arithmetic, body(): jax.ops.segment_sum(expanded - unbin_local(apply_local_map), base_index,...  114 us
    psum x2, blocking collectives, squares(): return lax.psum(jnp.sum(residual_vector * residual_vector), ('det', 'obs'))  81.2 us
    scatter-add x1, other arithmetic, body(): jax.ops.segment_sum(cleaned, base_index, num_segments=nbase, indices_are_...  57.2 us
    mul x2, other arithmetic, body(): expanded * cos_w  51.5 us
    all_to_all x1, waiting for transfers between devices, body(): lax.all_to_all(pack_map(first_total), 'obs', split_axis=0, concat_axis=0,...  50 us
    all_to_all x2, blocking collectives, body(): lax.all_to_all(pack_map(apply_total), 'obs', split_axis=0, concat_axis=0,...  47.4 us
  transfers between devices with their start and end apart: 6, of which 4 were waited for; matrix products, arithmetic and copies ran while one was open for 30% of the time, Pallas kernels for 0%

commit v1 on v0

--- a/solution.py
+++ b/solution.py
@@ -50,7 +50,9 @@
 
 
 def combine_det(partial_value):
-    total = lax.psum(partial_value, "det")
+    total = partial_value
+    for hop in (1, 2):
+        total = total + lax.ppermute(total, "det", [(dev, dev ^ hop) for dev in range(4)])
     return total
 
 

time: 1080 us -> 1020 us (0.944)
  waiting for transfers between devices: 187 us -> 133 us
  between operations: 19 us -> 5.53 us
    psum x3 -> x0, waiting for transfers between devices: 137 us -> none  [combine_det(): total = lax.psum(partial_value, 'det')]
    ppermute x0 -> x6, waiting for transfers between devices: none -> 83.1 us  [combine_det(): lax.ppermute(total, 'det', [(dev, dev ^ hop) for dev in range(4)])]
  transfers between devices with their start and end apart: 6 -> 9, of which waited for: 4 -> 7; matrix products, arithmetic and copies ran while one was open for 30% -> 32% of each run, Pallas kernels for 0% -> 0%
where the time goes in v1:
time: 1020 us; the launch traced here: 1010 us
  other arithmetic  538 us (53%)
  blocking collectives  217 us (21%)
  waiting for transfers between devices  133 us (13%)
  local copies, waits for them, and re-layouts  58.8 us (6%)
  matrix products  33.8 us (3%)
  starting transfers between devices  24.9 us (2%)
    select_n x12, other arithmetic, body(): jnp.searchsorted(ends, jnp.arange(samples, dtype=jnp.int32), side='right')  301 us
    scatter-add x2, other arithmetic, body(): jax.ops.segment_sum(expanded - unbin_local(apply_local_map), base_index,...  114 us
    ppermute x6, waiting for transfers between devices, combine_det(): lax.ppermute(total, 'det', [(dev, dev ^ hop) for dev in range(4)])  83.1 us
    psum x2, blocking collectives, squares(): return lax.psum(jnp.sum(residual_vector * residual_vector), ('det', 'obs'))  81.1 us
    scatter-add x1, other arithmetic, body(): jax.ops.segment_sum(cleaned, base_index, num_segments=nbase, indices_are_...  57 us
    mul x2, other arithmetic, body(): expanded * cos_w  52 us
    all_to_all x1, waiting for transfers between devices, body(): lax.all_to_all(pack_map(first_total), 'obs', split_axis=0, concat_axis=0,...  50 us
    all_to_all x2, blocking collectives, body(): lax.all_to_all(pack_map(apply_total), 'obs', split_axis=0, concat_axis=0,...  47.3 us
  transfers between devices with their start and end apart: 9, of which 7 were waited for; matrix products, arithmetic and copies ran while one was open for 32% of the time, Pallas kernels for 0%

profile of v1, /device:TPU:12, one launch (start us, length us, event | category | flops | bytes accessed | tf_op | source)
XLA Modules:
  0.0 1011.6 jit_solution(3214483252732387436)
XLA Ops:
  14.6 26.2 %collective-permute-done = f32[16,9,2048]{2,0,1:T(8,128)S(1)} collective-permute-done((f32[16,9,2048]{2,0,1:T(8,128)S(1)}, f32[16,9,2048]{2,0,1:T(8,128)S(1)}, u32[]{:S(2)}, u32[]{:S(2)}) %collective-permute-start) | collective-permute-done | bytes 1179680 | tf_op jit(solution)/shard_map/ppermute | solution.py:55
  48.5 20.0 %collective-permute-done.1 = f32[16,9,2048]{2,0,1:T(8,128)S(1)} collective-permute-done((f32[16,9,2048]{2,0,1:T(8,128)S(1)}, f32[16,9,2048]{2,0,1:T(8,128)S(1)}, u32[]{:S(2)}, u32[]{:S(2)}) %collective-permute-start.1) | collective-permute-done | bytes 1179680 | tf_op jit(solution)/shard_map/ppermute | solution.py:55
  78.5 50.0 %all-to-all-done.1 = f32[8,4,9,2048]{3,1,2,0:T(4,128)S(1)} async-done(((f32[8,4,9,2048]{3,1,2,0:T(4,128)}), f32[8,4,9,2048]{3,1,2,0:T(4,128)S(1)}, u32[]{:S(2)}, u32[]{:S(2)}) %all-to-all-start.1) | async-done | bytes 2359328 | tf_op jit(solution)/shard_map/all_to_all | solution.py:179
  144.9 313.9 %while.24 = (s32[]{:T(128)}, u32[8192]{0:T(1024)S(1)}, u32[8192]{0:T(1024)S(1)}, s32[40]{0:T(128)S(1)}, s32[]{:T(128)}, /*index=5*/s32[]{:T(128)}) while((s32[]{:T(128)}, u32[8192]{0:T(1024)S(1)}, u32[8192]{0:T(1024)S(1)}, s32[40]{0:T(128)S(1)}, s32[]{:T(128)}, /*index=5*/s32[]{:T(128)}) %tuple.233), condition=%wide.region_2.3_spmd.clone, body=%wide.region_1.2_spmd.clone.sunk | while | flops 1392643 | bytes 262864 | solution.py:82
  147.1 25.1 %fusion.141 = u32[8192]{0:T(1024)S(1)} fusion(u32[8192]{0:T(1024)S(1)} %get-tuple-element.525, u32[8192]{0:T(1024)S(1)} %get-tuple-element.524, s32[]{:T(128)} %bitcast.468, s32[]{:T(128)} %bitcast.469, s32[]{:T(128)} %bitcast.470, s32[]{:T(128)} %bitcast.471, s32[]{:T(128)} %bitcast.472, s32[]{:T(128)} %bitcast.473, s32[]{:T(128)} %bitcast.474, ...), kind=kLoop, calls=%fused_computation.8.clone.1 | loop fusion | flops 696320 | bytes 98465 | tf_op jit(solution)/shard_map/jit(searchsorted)/jit(_searchsorted_scan_impl)/vmap(jit(_searchsorted_scan_impl))/while/body/eval_jaxpr/select_n | solution.py:82
  172.1 25.1 %fusion.140 = u32[8192]{0:T(1024)S(1)} fusion(u32[8192]{0:T(1024)S(1)} %get-tuple-element.525, u32[8192]{0:T(1024)S(1)} %get-tuple-element.524, s32[]{:T(128)} %bitcast.468, s32[]{:T(128)} %bitcast.469, s32[]{:T(128)} %bitcast.470, s32[]{:T(128)} %bitcast.471, s32[]{:T(128)} %bitcast.472, s32[]{:T(128)} %bitcast.473, s32[]{:T(128)} %bitcast.474, ...), kind=kLoop, calls=%fused_computation.9.clone.1 | loop fusion | flops 696320 | bytes 98465 | tf_op jit(solution)/shard_map/jit(searchsorted)/jit(_searchsorted_scan_impl)/vmap(jit(_searchsorted_scan_impl))/while/body/eval_jaxpr/select_n | solution.py:82
  199.4 25.1 %fusion.141 = u32[8192]{0:T(1024)S(1)} fusion(u32[8192]{0:T(1024)S(1)} %get-tuple-element.525, u32[8192]{0:T(1024)S(1)} %get-tuple-element.524, s32[]{:T(128)} %bitcast.468, s32[]{:T(128)} %bitcast.469, s32[]{:T(128)} %bitcast.470, s32[]{:T(128)} %bitcast.471, s32[]{:T(128)} %bitcast.472, s32[]{:T(128)} %bitcast.473, s32[]{:T(128)} %bitcast.474, ...), kind=kLoop, calls=%fused_computation.8.clone.1 | loop fusion | flops 696320 | bytes 98465 | tf_op jit(solution)/shard_map/jit(searchsorted)/jit(_searchsorted_scan_impl)/vmap(jit(_searchsorted_scan_impl))/while/body/eval_jaxpr/select_n | solution.py:82
  224.5 25.1 %fusion.140 = u32[8192]{0:T(1024)S(1)} fusion(u32[8192]{0:T(1024)S(1)} %get-tuple-element.525, u32[8192]{0:T(1024)S(1)} %get-tuple-element.524, s32[]{:T(128)} %bitcast.468, s32[]{:T(128)} %bitcast.469, s32[]{:T(128)} %bitcast.470, s32[]{:T(128)} %bitcast.471, s32[]{:T(128)} %bitcast.472, s32[]{:T(128)} %bitcast.473, s32[]{:T(128)} %bitcast.474, ...), kind=kLoop, calls=%fused_computation.9.clone.1 | loop fusion | flops 696320 | bytes 98465 | tf_op jit(solution)/shard_map/jit(searchsorted)/jit(_searchsorted_scan_impl)/vmap(jit(_searchsorted_scan_impl))/while/body/eval_jaxpr/select_n | solution.py:82
  251.7 25.1 %fusion.141 = u32[8192]{0:T(1024)S(1)} fusion(u32[8192]{0:T(1024)S(1)} %get-tuple-element.525, u32[8192]{0:T(1024)S(1)} %get-tuple-element.524, s32[]{:T(128)} %bitcast.468, s32[]{:T(128)} %bitcast.469, s32[]{:T(128)} %bitcast.470, s32[]{:T(128)} %bitcast.471, s32[]{:T(128)} %bitcast.472, s32[]{:T(128)} %bitcast.473, s32[]{:T(128)} %bitcast.474, ...), kind=kLoop, calls=%fused_computation.8.clone.1 | loop fusion | flops 696320 | bytes 98465 | tf_op jit(solution)/shard_map/jit(searchsorted)/jit(_searchsorted_scan_impl)/vmap(jit(_searchsorted_scan_impl))/while/body/eval_jaxpr/select_n | solution.py:82
  276.8 25.1 %fusion.140 = u32[8192]{0:T(1024)S(1)} fusion(u32[8192]{0:T(1024)S(1)} %get-tuple-element.525, u32[8192]{0:T(1024)S(1)} %get-tuple-element.524, s32[]{:T(128)} %bitcast.468, s32[]{:T(128)} %bitcast.469, s32[]{:T(128)} %bitcast.470, s32[]{:T(128)} %bitcast.471, s32[]{:T(128)} %bitcast.472, s32[]{:T(128)} %bitcast.473, s32[]{:T(128)} %bitcast.474, ...), kind=kLoop, calls=%fused_computation.9.clone.1 | loop fusion | flops 696320 | bytes 98465 | tf_op jit(solution)/shard_map/jit(searchsorted)/jit(_searchsorted_scan_impl)/vmap(jit(_searchsorted_scan_impl))/while/body/eval_jaxpr/select_n | solution.py:82
  304.0 25.1 %fusion.141 = u32[8192]{0:T(1024)S(1)} fusion(u32[8192]{0:T(1024)S(1)} %get-tuple-element.525, u32[8192]{0:T(1024)S(1)} %get-tuple-element.524, s32[]{:T(128)} %bitcast.468, s32[]{:T(128)} %bitcast.469, s32[]{:T(128)} %bitcast.470, s32[]{:T(128)} %bitcast.471, s32[]{:T(128)} %bitcast.472, s32[]{:T(128)} %bitcast.473, s32[]{:T(128)} %bitcast.474, ...), kind=kLoop, calls=%fused_computation.8.clone.1 | loop fusion | flops 696320 | bytes 98465 | tf_op jit(solution)/shard_map/jit(searchsorted)/jit(_searchsorted_scan_impl)/vmap(jit(_searchsorted_scan_impl))/while/body/eval_jaxpr/select_n | solution.py:82
  329.1 25.1 %fusion.140 = u32[8192]{0:T(1024)S(1)} fusion(u32[8192]{0:T(1024)S(1)} %get-tuple-element.525, u32[8192]{0:T(1024)S(1)} %get-tuple-element.524, s32[]{:T(128)} %bitcast.468, s32[]{:T(128)} %bitcast.469, s32[]{:T(128)} %bitcast.470, s32[]{:T(128)} %bitcast.471, s32[]{:T(128)} %bitcast.472, s32[]{:T(128)} %bitcast.473, s32[]{:T(128)} %bitcast.474, ...), kind=kLoop, calls=%fused_computation.9.clone.1 | loop fusion | flops 696320 | bytes 98465 | tf_op jit(solution)/shard_map/jit(searchsorted)/jit(_searchsorted_scan_impl)/vmap(jit(_searchsorted_scan_impl))/while/body/eval_jaxpr/select_n | solution.py:82
  356.3 25.1 %fusion.141 = u32[8192]{0:T(1024)S(1)} fusion(u32[8192]{0:T(1024)S(1)} %get-tuple-element.525, u32[8192]{0:T(1024)S(1)} %get-tuple-element.524, s32[]{:T(128)} %bitcast.468, s32[]{:T(128)} %bitcast.469, s32[]{:T(128)} %bitcast.470, s32[]{:T(128)} %bitcast.471, s32[]{:T(128)} %bitcast.472, s32[]{:T(128)} %bitcast.473, s32[]{:T(128)} %bitcast.474, ...), kind=kLoop, calls=%fused_computation.8.clone.1 | loop fusion | flops 696320 | bytes 98465 | tf_op jit(solution)/shard_map/jit(searchsorted)/jit(_searchsorted_scan_impl)/vmap(jit(_searchsorted_scan_impl))/while/body/eval_jaxpr/select_n | solution.py:82
  381.4 25.1 %fusion.140 = u32[8192]{0:T(1024)S(1)} fusion(u32[8192]{0:T(1024)S(1)} %get-tuple-element.525, u32[8192]{0:T(1024)S(1)} %get-tuple-element.524, s32[]{:T(128)} %bitcast.468, s32[]{:T(128)} %bitcast.469, s32[]{:T(128)} %bitcast.470, s32[]{:T(128)} %bitcast.471, s32[]{:T(128)} %bitcast.472, s32[]{:T(128)} %bitcast.473, s32[]{:T(128)} %bitcast.474, ...), kind=kLoop, calls=%fused_computation.9.clone.1 | loop fusion | flops 696320 | bytes 98465 | tf_op jit(solution)/shard_map/jit(searchsorted)/jit(_searchsorted_scan_impl)/vmap(jit(_searchsorted_scan_impl))/while/body/eval_jaxpr/select_n | solution.py:82
  408.7 25.1 %fusion.141 = u32[8192]{0:T(1024)S(1)} fusion(u32[8192]{0:T(1024)S(1)} %get-tuple-element.525, u32[8192]{0:T(1024)S(1)} %get-tuple-element.524, s32[]{:T(128)} %bitcast.468, s32[]{:T(128)} %bitcast.469, s32[]{:T(128)} %bitcast.470, s32[]{:T(128)} %bitcast.471, s32[]{:T(128)} %bitcast.472, s32[]{:T(128)} %bitcast.473, s32[]{:T(128)} %bitcast.474, ...), kind=kLoop, calls=%fused_computation.8.clone.1 | loop fusion | flops 696320 | bytes 98465 | tf_op jit(solution)/shard_map/jit(searchsorted)/jit(_searchsorted_scan_impl)/vmap(jit(_searchsorted_scan_impl))/while/body/eval_jaxpr/select_n | solution.py:82
  433.8 25.1 %fusion.140 = u32[8192]{0:T(1024)S(1)} fusion(u32[8192]{0:T(1024)S(1)} %get-tuple-element.525, u32[8192]{0:T(1024)S(1)} %get-tuple-element.524, s32[]{:T(128)} %bitcast.468, s32[]{:T(128)} %bitcast.469, s32[]{:T(128)} %bitcast.470, s32[]{:T(128)} %bitcast.471, s32[]{:T(128)} %bitcast.472, s32[]{:T(128)} %bitcast.473, s32[]{:T(128)} %bitcast.474, ...), kind=kLoop, calls=%fused_computation.9.clone.1 | loop fusion | flops 696320 | bytes 98465 | tf_op jit(solution)/shard_map/jit(searchsorted)/jit(_searchsorted_scan_impl)/vmap(jit(_searchsorted_scan_impl))/while/body/eval_jaxpr/select_n | solution.py:82
  474.4 57.0 %scatter_custom_fusion = f32[40]{0:T(128)S(1)} fusion(s32[8192]{0:T(1024)S(1)} %convert_element_type.34, f32[8192]{0:T(1024)S(1)} %add_subtract_fusion.2, f32[]{:T(128)} %constant.148.clone.1), kind=kCustom, calls=%fused_computation.233 | custom fusion | flops 8192 | bytes 164 | tf_op jit(solution)/shard_map/scatter-add | solution.py:204
  533.5 26.0 %fusion.114 = (f32[8192]{0:T(1024)S(1)}, f32[8192]{0:T(1024)S(1)}, pred[8192]{0:T(1024)(128)(4,1)S(1)}, pred[8192]{0:T(1024)(128)(4,1)S(1)}, pred[8192]{0:T(1024...) fusion(f32[8192]{0:T(1024)S(1)} %bitcast.527, ...), kind=kLoop, calls=%fused_computation.238 | loop fusion | flops 712704 | bytes 458912 | tf_op jit(solution)/shard_map/mul | solution.py:213
  568.1 9.6 collective-permute-done.2
  579.6 9.8 collective-permute-done.3
  589.9 24.0 %all_to_all.36 = f32[8,4,3,2048]{3,1,2,0:T(4,128)S(1)} all-to-all(f32[8,4,3,2048]{3,1,2,0:T(4,128)S(1)} %fusion.51), channel_id=1, replica_groups=mesh['det'=4,'obs'=8] {'obs'}, dimensions={0} | all-to-all | bytes 1572864 | tf_op jit(solution)/shard_map/all_to_all | solution.py:215
  617.2 23.4 %all_to_all.37 = f32[8,4,3,2048]{3,1,2,0:T(4,128)S(1)} all-to-all(f32[8,4,3,2048]{3,1,2,0:T(4,128)S(1)} %fusion.15), channel_id=1, replica_groups=mesh['det'=4,'obs'=8] {'obs'}, dimensions={0} | all-to-all | bytes 1572864 | tf_op jit(solution)/shard_map/all_to_all | solution.py:197
  654.9 57.2 %scatter_custom_fusion.1 = f32[40]{0:T(128)S(1)} fusion(s32[8192]{0:T(1024)} %copy-done.1, f32[8192]{0:T(1024)S(1)} %add_subtract_fusion.1, f32[]{:T(128)} %constant.148.clone.1), kind=kCustom, calls=%fused_computation.231 | custom fusion | flops 8192 | bytes 672 | tf_op jit(solution)/shard_map/scatter-add | solution.py:220
  712.7 42.1 %all-reduce = (f32[]{:T(128)}, f32[]{:T(128)}) all-reduce(f32[]{:T(128)} %get-tuple-element.196, f32[]{:T(128)} %get-tuple-element.195), channel_id=1, replica_groups=mesh['det'=4,'obs'=8] {'det','obs'}, use_global_device_ids=true, to_apply=%region_7.9 | all-reduce | flops 2 | bytes 16 | tf_op jit(solution)/shard_map/psum | solution.py:60
  756.8 38.9 %psum.30 = f32[]{:T(128)} all-reduce(f32[]{:T(128)} %get-tuple-element.209), channel_id=1, replica_groups=mesh['det'=4,'obs'=8] {'det','obs'}, use_global_device_ids=true, to_apply=%region_12.15 | all-reduce | flops 1 | bytes 8 | tf_op jit(solution)/shard_map/psum | solution.py:60
  799.1 26.0 %fusion.113 = (f32[8192]{0:T(1024)S(1)}, f32[8192]{0:T(1024)S(1)}) fusion(f32[8192]{0:T(1024)S(1)} %bitcast.529, pred[8192]{0:T(1024)(128)(4,1)} %get-tuple-element.252, pred[8192]{0:T(1024)(128)(4,1)} %get-tuple-element.251, pred[8192]{0:T(1024)(128)(4,1)} %get-tuple-element.250, pred[8192]{0:T(1024)(128)(4,1)} %get-tuple-element.249, ...), kind=kLoop, calls=%fused_computation.237 | loop fusion | flops 335872 | bytes 426144 | tf_op jit(solution)/shard_map/mul | solution.py:213
  833.7 8.6 collective-permute-done.4
  843.9 9.0 collective-permute-done.5
  853.5 23.3 %all_to_all.38 = f32[8,4,3,2048]{3,1,2,0:T(4,128)S(1)} all-to-all(f32[8,4,3,2048]{3,1,2,0:T(4,128)S(1)} %fusion.49), channel_id=1, replica_groups=mesh['det'=4,'obs'=8] {'obs'}, dimensions={0} | all-to-all | bytes 1572864 | tf_op jit(solution)/shard_map/all_to_all | solution.py:215
  880.1 23.6 %all_to_all.39 = f32[8,4,3,2048]{3,1,2,0:T(4,128)S(1)} all-to-all(f32[8,4,3,2048]{3,1,2,0:T(4,128)S(1)} %fusion.13), channel_id=1, replica_groups=mesh['det'=4,'obs'=8] {'obs'}, dimensions={0} | all-to-all | bytes 1572864 | tf_op jit(solution)/shard_map/all_to_all | solution.py:197
  909.8 57.2 %scatter_custom_fusion.2 = f32[40]{0:T(128)S(1)} fusion(s32[8192]{0:T(1024)} %copy-done.1, f32[8192]{0:T(1024)S(1)} %add_subtract_fusion, f32[]{:T(128)} %constant.148.clone.1), kind=kCustom, calls=%fused_computation.229 | custom fusion | flops 8192 | bytes 672 | tf_op jit(solution)/shard_map/scatter-add | solution.py:220
  967.6 41.3 %psum.31 = f32[]{:T(128)} all-reduce(f32[]{:T(128)} %multiply_reduce_fusion), channel_id=1, replica_groups=mesh['det'=4,'obs'=8] {'det','obs'}, use_global_device_ids=true, to_apply=%region_15.18 | all-reduce | flops 1 | bytes 8 | tf_op jit(solution)/shard_map/psum | solution.py:226
  (182 shorter events, 131.7 us)
Async XLA Ops:
  0.6 7.0 copy-start.8
  12.3 2.3 copy-start.11
  13.0 27.8 %collective-permute-start = (f32[16,9,2048]{2,0,1:T(8,128)S(1)}, f32[16,9,2048]{2,0,1:T(8,128)S(1)}, u32[]{:S(2)}, u32[]{:S(2)}) collective-permute-start(f32[16,9,2048]{2,0,1:T(8,128)S(1)} %copy.175), channel_id=1, source_target_pairs={{0,8},{8,0},{16,24},{24,16},{1,9},{9,1},{17,25},{25,17},{2,10},{10... | collective-permute-start | bytes 3538952 | tf_op jit(solution)/shard_map/ppermute | solution.py:55
  41.6 26.9 %collective-permute-start.1 = (f32[16,9,2048]{2,0,1:T(8,128)S(1)}, f32[16,9,2048]{2,0,1:T(8,128)S(1)}, u32[]{:S(2)}, u32[]{:S(2)}) collective-permute-start(f32[16,9,2048]{2,0,1:T(8,128)S(1)} %copy_add_fusion.2), channel_id=1, source_target_pairs={{0,16},{8,24},{16,0},{24,8},{1,17},{9,25},{17,1},{25,9},{2,18},{10... | collective-permute-start | bytes 3538952 | tf_op jit(solution)/shard_map/ppermute | solution.py:55
  43.1 28.5 %all-to-all-start = ((s32[8,1,4]{2,1,0:T(1,128)}), s32[8,1,4]{2,1,0:T(1,128)S(1)}, u32[]{:S(2)}, u32[]{:S(2)}) async-start(s32[8,1,4]{2,1,0:T(1,128)} %bitcast.10), calls=%async_computation | async-start | bytes 8192 | tf_op jit(solution)/shard_map/all_to_all | solution.py:180
  71.7 5.7 copy-start.9
  71.7 56.8 %all-to-all-start.1 = ((f32[8,4,9,2048]{3,1,2,0:T(4,128)}), f32[8,4,9,2048]{3,1,2,0:T(4,128)S(1)}, u32[]{:S(2)}, u32[]{:S(2)}) async-start(f32[8,4,9,2048]{3,1,2,0:T(4,128)} %fusion.34), calls=%async_computation.1 | async-start | bytes 4718592 | tf_op jit(solution)/shard_map/all_to_all | solution.py:179
  137.1 321.8 %all-to-all-start.2 = ((f32[8,4,3,2048]{3,1,2,0:T(4,128)}), f32[8,4,3,2048]{3,1,2,0:T(4,128)}, u32[]{:S(2)}, u32[]{:S(2)}) async-start(f32[8,4,3,2048]{3,1,2,0:T(4,128)} %fusion.17), calls=%async_computation.2 | async-start | bytes 1572864 | tf_op jit(solution)/shard_map/all_to_all | solution.py:197
  458.9 15.6 %copy-start.1 = (s32[8192]{0:T(1024)}, s32[8192]{0:T(1024)S(1)}, u32[]{:S(2)}) copy-start(s32[8192]{0:T(1024)S(1)} %convert_element_type.34) | copy-start | bytes 98308
  458.9 193.3 %copy-start.2 = (s32[1024]{0:T(1024)}, s32[1024]{0:T(1024)S(1)}, u32[]{:S(2)}) copy-start(s32[1024]{0:T(1024)S(1)} %pad_clamp_fusion) | copy-start | bytes 12292
  458.9 14.4 %copy-start.3 = (pred[32]{0:T(512)(128)(4,1)}, pred[32]{0:T(512)(128)(4,1)S(1)}, u32[]{:S(2)}) copy-start(pred[32]{0:T(512)(128)(4,1)S(1)} %compare_and_fusion.1) | copy-start | bytes 100
  469.3 5.1 copy-start
  566.5 11.2 %collective-permute-start.2 = (f32[16,3,2048]{2,0,1:T(8,128)S(1)}, f32[16,3,2048]{2,0,1:T(8,128)S(1)}, u32[]{:S(2)}, u32[]{:S(2)}) collective-permute-start(f32[16,3,2048]{2,0,1:T(8,128)S(1)} %copy.176), channel_id=1, source_target_pairs={{0,8},{8,0},{16,24},{24,16},{1,9},{9,1},{17,25},{25,17},{2,10},{10... | collective-permute-start | bytes 1179656 | tf_op jit(solution)/shard_map/ppermute | solution.py:55
  579.0 10.3 %collective-permute-start.3 = (f32[16,3,2048]{2,0,1:T(8,128)S(1)}, f32[16,3,2048]{2,0,1:T(8,128)S(1)}, u32[]{:S(2)}, u32[]{:S(2)}) collective-permute-start(f32[16,3,2048]{2,0,1:T(8,128)S(1)} %copy_add_fusion.1), channel_id=1, source_target_pairs={{0,16},{8,24},{16,0},{24,8},{1,17},{9,25},{17,1},{25,9},{2,18},{10... | collective-permute-start | bytes 1179656 | tf_op jit(solution)/shard_map/ppermute | solution.py:55
  648.3 5.6 copy-start.4
  756.8 42.3 %copy-start.6 = (f32[40]{0:T(128)}, f32[40]{0:T(128)S(1)}, u32[]{:S(2)}) copy-start(f32[40]{0:T(128)S(1)} %get-tuple-element.210) | copy-start | bytes 484
  832.1 10.2 %collective-permute-start.4 = (f32[16,3,2048]{2,0,1:T(8,128)S(1)}, f32[16,3,2048]{2,0,1:T(8,128)S(1)}, u32[]{:S(2)}, u32[]{:S(2)}) collective-permute-start(f32[16,3,2048]{2,0,1:T(8,128)S(1)} %copy.177), channel_id=1, source_target_pairs={{0,8},{8,0},{16,24},{24,16},{1,9},{9,1},{17,25},{25,17},{2,10},{10... | collective-permute-start | bytes 1179656 | tf_op jit(solution)/shard_map/ppermute | solution.py:55
  843.6 9.3 collective-permute-start.5
  906.9 1.9 copy-start.5
  907.5 102.8 %copy-start.7 = (f32[40]{0:T(128)S(1)}, f32[40]{0:T(128)}, u32[]{:S(2)}) copy-start(f32[40]{0:T(128)} %copy-done.6) | copy-start | bytes 484
  907.5 102.8 %copy-start.10 = (s32[1,1,40]{2,1,0:T(1,128)S(1)}, s32[1,1,40]{2,1,0:T(1,128)}, u32[]{:S(2)}) copy-start(s32[1,1,40]{2,1,0:T(1,128)} %param.16) | copy-start | bytes 484
